TPU v7x, 32 devices: a whole 2x2x4 slice. The times are simulated.
32 devices in a mesh: dp: 4 (over x, core), pipe: 8 (over z, y).
Axes of the slice: x: 2, y: 2, z: 4, core: 2. Of those that a mesh axis runs over, the one named last changes fastest.
Arguments:
- pre: bfloat16 [512, 49152], P('dp', 'pipe'), may hold values from -6 to 6
- grad_out: bfloat16 [512, 6144], P('dp', 'pipe'), may hold values from -6 to 6
- weight_slots: bfloat16 [8, 292, 128, 128], P('pipe', 'dp'), may hold values from -0.21875 to 0.21875
- block_rows: int32 [8, 292], P('pipe', 'dp'), may hold values from 0 to 47, as said below
- block_cols: int32 [8, 292], P('pipe', 'dp'), may hold values from 0 to 47, as said below
- block_count: int32 [8, 4], P('pipe', 'dp'), may hold values from 0 to 73, as said below
Outputs:
- pre_grad: bfloat16 [512, 49152], P('dp', 'pipe')
- weight_grad: bfloat16 [8, 292, 128, 128], P('pipe', 'dp')
Inputs may be any that keep to these rules, and one draw needn't show every extreme that they name: `block_rows`: live slots of slab p list each of its 48 rows of blocks exactly 6 times, with distinct columns; dead slots hold valid indices. `block_cols`: within a row of blocks the live columns are distinct. `block_count`: the counts of one slab sum to 288; in every slab some device holds exactly 73.
All inputs are finite; a program needn't handle non-finite values.
Results may differ from a plain program's by a relative error of at most 0.009.
Values may be sent and summed in bfloat16 or wider, within the bound.
A program may use at most 128 MiB of HBM per device.

v0:
```python
import jax
import jax.numpy as jnp
from jax import lax
from jax.sharding import PartitionSpec as P

BLOCK = 128
inv_root_two = 0.7071067811865476
inverse_square_root_tau = 0.3989422804014327


def gelu_parts(pre_wide):
    normal_cdf = 0.5 * (1.0 + jax.scipy.special.erf(pre_wide * inv_root_two))
    density = jnp.exp(-0.5 * pre_wide * pre_wide) * inverse_square_root_tau
    return (pre_wide * normal_cdf, normal_cdf + pre_wide * density)


def on_device(pre, grad_out, weight_slots, block_rows, block_cols, block_count):
    tok_rows = pre.shape[0]
    slab_rows = pre.shape[1] // BLOCK
    slot_cap = weight_slots.shape[1]
    whole_grad = lax.all_gather(grad_out, "pipe", axis=1, tiled=True)
    grad_blocks = whole_grad.reshape(tok_rows, -1, BLOCK)
    pre_wide = pre.astype(jnp.float32)
    activation, slopes = gelu_parts(pre_wide)
    activation = activation.astype(jnp.bfloat16)
    act_blocks = activation.reshape(tok_rows, slab_rows, BLOCK)
    row_range = jnp.arange(slab_rows)
    all_rows, all_cols, all_counts = (
        lax.all_gather(block_rows, "dp", axis=1, tiled=True),
        lax.all_gather(block_cols, "dp", axis=1, tiled=True),
        lax.all_gather(block_count, "dp", axis=1, tiled=True),
    )
    live_all = jnp.arange(all_rows.shape[1]) % slot_cap < jnp.repeat(all_counts[0], slot_cap)
    row_ids = all_rows[0]
    col_ids = all_cols[0]
    live_mask = live_all
    gradient_fragments = grad_blocks[:, col_ids, :]
    masked = (
        lax.all_gather(weight_slots, "dp", axis=1, tiled=True)[0]
        * live_mask.astype(jnp.bfloat16)[:, None, None]
    )
    value_portion = jnp.einsum(
        "tkd,khd->tkh", gradient_fragments, masked, preferred_element_type=jnp.float32
    )
    row_hot = (row_ids[:, None] == row_range[None, :]).astype(jnp.float32)
    hidden_grad = jnp.einsum("tkh,kr->trh", value_portion, row_hot)
    row_ids = all_rows[0]
    col_ids = all_cols[0]
    live_mask = live_all
    act_pieces = act_blocks[:, row_ids, :]
    gradient_fragments = grad_blocks[:, col_ids, :]
    grad_term = jnp.einsum(
        "tkh,tkd->khd", act_pieces, gradient_fragments, preferred_element_type=jnp.float32
    )
    own_grad = lax.psum_scatter(
        (grad_term * live_mask.astype(jnp.float32)[:, None, None]).astype(jnp.bfloat16),
        "dp",
        scatter_dimension=0,
        tiled=True,
    )
    weight_grad = own_grad[None]
    pre_grad = (hidden_grad.reshape(tok_rows, -1) * slopes).astype(jnp.bfloat16)
    return (pre_grad, weight_grad)


def solution(mesh):
    in_specs = (
        P("dp", "pipe"),
        P("dp", "pipe"),
        P("pipe", "dp", None, None),
        P("pipe", "dp"),
        P("pipe", "dp"),
        P("pipe", "dp"),
    )
    out_specs = (P("dp", "pipe"), P("pipe", "dp", None, None))
    return jax.shard_map(
        on_device, mesh=mesh, in_specs=in_specs, out_specs=out_specs, check_vma=False
    )
```

profile of v0, /device:TPU:0, one launch (start us, length us, event | category | flops | bytes accessed | tf_op | source)
XLA Modules:
  0.0 271.9 jit_solution(10886016366637159782)
XLA Ops:
  7.2 1.9 copy.18
  9.1 0.7 all-gather.3.cloned.1.call-update
  10.5 1.2 dynamic-slice
  12.4 0.7 bitcast_dynamic-update-slice_fusion.1
  13.1 0.8 bitcast_dynamic-update-slice_fusion
  13.9 0.7 bitcast_dynamic-update-slice_fusion.2
  14.6 6.4 %all-reduce.3 = (s32[292]{0:T(512)S(1)}, s32[4]{0:T(128)S(1)}, s32[292]{0:T(512)S(1)}) all-reduce(s32[292]{0:T(512)S(1)} %bitcast_dynamic-update-slice_fusion, s32[4]{0:T(128)S(1)} %bitcast_dynamic-update-slice_fusion.1, s32[292]{0:T(512)S(1)} %bitcast_dynamic-update-slice_fusion.2), channel_id=1, replica_groups=mesh['dp'=4,'pipe'=8] {'dp'}, use_global_device_ids=true, to_apply=%add.2 | all-reduce | flops 588 | bytes 4704
  21.1 0.1 reshape.94
  21.3 1.6 copy.21
  22.9 34.8 %all-gather.5.cloned.1.call-done = bf16[128,6144]{0,1:T(8,128)(2,1)} async-done(((bf16[128,768]{0,1:T(8,128)(2,1)}), bf16[128,6144]{0,1:T(8,128)(2,1)}) %all-gather.5.cloned.1.call-update) | async-done | bytes 1572880 | tf_op jit(solution)/shard_map/all_gather | solution.py:21
  57.7 1.9 copy.19
  59.6 11.1 %gather_fusion = bf16[292,128,128]{2,1,0:T(8,128)(2,1)} fusion(bf16[128,48,128]{2,0,1:T(8,128)(2,1)S(1)} %copy.19, s32[1024]{0:T(1024)S(1)} %pad_clamp_fusion.1), kind=kCustom, calls=%fused_computation | custom fusion | bytes 19137680 | tf_op jit(solution)/shard_map/gather | solution.py:37
  70.7 51.8 %all-gather.3.cloned.1.call-done = bf16[1,292,128,128]{3,2,0,1:T(8,128)(2,1)} async-done(((bf16[1,73,128,128]{3,2,0,1:T(8,128)(2,1)}), bf16[1,292,128,128]{3,2,0,1:T(8,128)(2,1)}) %all-gather.3.cloned.1.call-update) | async-done | bytes 9568272 | tf_op jit(solution)/shard_map/all_gather | solution.py:39
  122.6 12.9 %fusion.5 = bf16[128,292,128]{0,2,1:T(8,128)(2,1)} fusion(bf16[292,128,128]{2,1,0:T(8,128)(2,1)} %gather_fusion, bf16[1,292,128,128]{3,2,0,1:T(8,128)(2,1)} %all-gather.3.cloned.1.call-done, bf16[292]{0:T(512)(128)(2,1)S(1)} %convert_element_type.27), kind=kOutput, calls=%fused_computation.9 | convolution fusion | flops 1229520896 | bytes 28705352 | tf_op jit(solution)/shard_map/tkd,khd->tkh/dot_general | solution.py:42
  135.5 13.7 %copy.20 = bf16[128,292,128]{2,1,0:T(8,128)(2,1)} copy(bf16[128,292,128]{0,2,1:T(8,128)(2,1)} %fusion.5) | data formatting | bytes 19136512 | tf_op jit(solution)/shard_map/tkd,khd->tkh/transpose | solution.py:42
  149.2 7.5 %convolution_bitcast_fusion = f32[128,48,128]{2,1,0:T(8,128)} fusion(bf16[128,292,128]{2,1,0:T(8,128)(2,1)} %copy.20, s32[292]{0:T(512)S(1)} %get-tuple-element.8), kind=kOutput, calls=%fused_computation.25 | convolution fusion | flops 459290304 | bytes 12715152 | tf_op jit(solution)/shard_map/tkh,kr->trh/dot_general | solution.py:46
  156.6 2.4 copy.27
  159.1 4.0 %fusion.21 = (bf16[128,6144]{0,1:T(8,128)(2,1)}, bf16[128,6144]{0,1:T(8,128)(2,1)}) fusion(bf16[128,6144]{0,1:T(8,128)(2,1)} %copy.21, f32[128,48,128]{0,2,1:T(8,128)S(1)} %copy.27), kind=kLoop, calls=%fused_computation.24 | loop fusion | flops 10223616 | bytes 7864320 | tf_op jit(solution)/shard_map/convert_element_type | solution.py:25
  163.0 1.9 copy.23
  164.9 10.5 %gather_fusion.1 = bf16[292,128,128]{2,1,0:T(8,128)(2,1)} fusion(bf16[128,48,128]{2,0,1:T(8,128)(2,1)S(1)} %copy.23, s32[1024]{0:T(1024)S(1)} %pad_clamp_fusion), kind=kCustom, calls=%fused_computation.1 | custom fusion | bytes 19137680 | tf_op jit(solution)/shard_map/gather | solution.py:50
  175.4 11.1 %multiply_convert_fusion = bf16[292,128,128]{2,1,0:T(8,128)(2,1)} fusion(f32[292]{0:T(512)S(1)} %get-tuple-element.9, bf16[292,128,128]{2,1,0:T(8,128)(2,1)} %gather_fusion, bf16[292,128,128]{2,1,0:T(8,128)(2,1)} %gather_fusion.1), kind=kOutput, calls=%fused_computation.2 | convolution fusion | flops 1234305024 | bytes 28705936 | tf_op jit(solution)/shard_map/tkh,tkd->khd/dot_general | solution.py:52
  186.5 1.4 copy-done
  187.9 1.6 copy.25
  189.4 76.0 %reduce-scatter.2.cloned.1.call-done = bf16[73,128,128]{2,1,0:T(8,128)(2,1)} async-done(((bf16[292,128,128]{2,1,0:T(8,128)(2,1)}), bf16[73,128,128]{2,1,0:T(8,128)(2,1)}) %reduce-scatter.2.cloned.1.call-update) | async-done | bytes 2392080 | tf_op jit(solution)/shard_map/reduce_scatter | solution.py:55
  (18 shorter events, 0.3 us)
Async XLA Ops:
  7.2 14.1 %copy-start.1 = (bf16[128,6144]{1,0:T(8,128)(2,1)S(1)}, bf16[128,6144]{1,0:T(8,128)(2,1)}, u32[]{:S(2)}) copy-start(bf16[128,6144]{1,0:T(8,128)(2,1)} %param.6) | copy-start | bytes 4718596
  7.2 50.5 %all-gather.5.cloned.1.call-start = ((), (), s32[]{:S(2)}) async-start(), calls=%async_computation.2 | async-start | bytes 1769472 | tf_op jit(solution)/shard_map/all_gather | solution.py:21
  9.1 113.5 %all-gather.3.cloned.1.call-start = ((), (), s32[]{:S(2)}) async-start(), calls=%async_computation.1 | async-start | bytes 11960320 | tf_op jit(solution)/shard_map/all_gather | solution.py:39
  9.8 255.6 %reduce-scatter.2.cloned.1.call-start = ((), (), s32[]{:S(2)}) async-start(), calls=%async_computation.3 | async-start | bytes 11960320 | tf_op jit(solution)/shard_map/reduce_scatter | solution.py:55
  186.5 1.4 copy-start
Sparse Core Ops, SparseCore 0:
  10.7 46.8 all-gather.4
  59.2 63.3 all-gather.2
  186.6 78.7 reduce-scatter.1
where the time goes:
time: 273 us; the launch traced here: 272 us
  waiting for transfers between devices  163 us (60%)
  local copies, waits for them, and re-layouts  51.4 us (19%)
  matrix products  31.5 us (12%)
  between operations  15.1 us (6%)
  blocking collectives  6.44 us (2%)
  other arithmetic  4.04 us (1%)
    reduce_scatter x1, waiting for transfers between devices, on_device(): lax.psum_scatter((grad_term * live_mask.astype(jnp.float32)[:, None, None...  76 us
    all_gather x1, waiting for transfers between devices, on_device(): lax.all_gather(weight_slots, 'dp', axis=1, tiled=True)[0]  51.8 us
    all_gather x1, waiting for transfers between devices, on_device(): whole_grad = lax.all_gather(grad_out, 'pipe', axis=1, tiled=True)  34.8 us
    transpose x1, local copies, waits for them, and re-layouts, on_device(): jnp.einsum('tkd,khd->tkh', gradient_fragments, masked, preferred_element_...  13.7 us
    dot_general x1, matrix products, on_device(): jnp.einsum('tkd,khd->tkh', gradient_fragments, masked, preferred_element_...  12.9 us
    gather x1, local copies, waits for them, and re-layouts, on_device(): gradient_fragments = grad_blocks[:, col_ids, :]  11.1 us
    dot_general x1, matrix products, on_device(): jnp.einsum('tkh,tkd->khd', act_pieces, gradient_fragments, preferred_elem...  11.1 us
    gather x1, local copies, waits for them, and re-layouts, on_device(): act_pieces = act_blocks[:, row_ids, :]  10.5 us
  transfers between devices with their start and end apart: 3, of which 3 were waited for; matrix products, arithmetic and copies ran while one was open for 7% of the time, Pallas kernels for 0%

commit v1 on v0

--- a/solution.py
+++ b/solution.py
@@ -6,6 +6,29 @@
 BLOCK = 128
 inv_root_two = 0.7071067811865476
 inverse_square_root_tau = 0.3989422804014327
+
+
+def register_record(s0, axis_name):
+    value_now = lax.axis_size(axis_name)
+    piece_out, tmp, x_new = (value_now, lax.axis_index(axis_name), s0.shape[1])
+    raw_out = low = s0
+    z2 = lax.dynamic_update_slice_in_dim(
+        jnp.zeros([s * piece_out if j == 1 else s for j, s in enumerate(s0.shape)], s0.dtype),
+        s0,
+        tmp * x_new,
+        axis=1,
+    )
+    for p in range(1, piece_out // 2 + 1):
+        raw_out = lax.ppermute(
+            raw_out, axis_name, list(map(lambda j: (j, (j + 1) % piece_out), range(piece_out)))
+        )
+        z2 = lax.dynamic_update_slice_in_dim(z2, raw_out, (tmp - p) % piece_out * x_new, axis=1)
+        if 2 * p < piece_out:
+            low = lax.ppermute(
+                low, axis_name, list(map(lambda j: (j, (j - 1) % piece_out), range(piece_out)))
+            )
+            z2 = lax.dynamic_update_slice_in_dim(z2, low, (tmp + p) % piece_out * x_new, axis=1)
+    return z2
 
 
 def gelu_parts(pre_wide):
@@ -18,7 +41,7 @@
     tok_rows = pre.shape[0]
     slab_rows = pre.shape[1] // BLOCK
     slot_cap = weight_slots.shape[1]
-    whole_grad = lax.all_gather(grad_out, "pipe", axis=1, tiled=True)
+    whole_grad = register_record(grad_out, "pipe")
     grad_blocks = whole_grad.reshape(tok_rows, -1, BLOCK)
     pre_wide = pre.astype(jnp.float32)
     activation, slopes = gelu_parts(pre_wide)

time: 273 us -> 227 us (0.83)
  waiting for transfers between devices: 163 us -> 102 us
  starting transfers between devices: 0.12 us -> 18.7 us
    all_gather x1, waiting for transfers between devices: 51.8 us -> 12.6 us  [on_device(): lax.all_gather(weight_slots, 'dp', axis=1, tiled=True)[0]]
    all_gather x1 -> x0, waiting for transfers between devices: 34.8 us -> none  [on_device(): whole_grad = lax.all_gather(grad_out, 'pipe', axis=1, tiled=True)]
    ppermute x0 -> x7, starting transfers between devices: none -> 18.7 us  [the longest x3 11.4 us: register_record(): lax.ppermute(low, axis_name, list(map(lambda j: (j, (j - 1) % piece_out),...]
    ppermute x0 -> x7, waiting for transfers between devices: none -> 12.7 us  [the longest x4 12.7 us: register_record(): lax.ppermute(raw_out, axis_name, list(map(lambda j: (j, (j + 1) % piece_o...]
    unnamed x14 -> x18, local copies, waits for them, and re-layouts: 9.78 us -> 9.04 us
  transfers between devices with their start and end apart: 3 -> 9, of which waited for: 3 -> 5; matrix products, arithmetic and copies ran while one was open for 7% -> 9% of each run, Pallas kernels for 0% -> 0%
where the time goes in v1:
time: 227 us
  waiting for transfers between devices  102 us (45%)
  local copies, waits for them, and re-layouts  50.2 us (22%)
  matrix products  31.4 us (14%)
  starting transfers between devices  18.7 us (8%)
  between operations  15.5 us (7%)
  blocking collectives  5.06 us (2%)
  other arithmetic  4.02 us (2%)
    reduce_scatter x1, waiting for transfers between devices, on_device(): lax.psum_scatter((grad_term * live_mask.astype(jnp.float32)[:, None, None...  75.8 us
    transpose x1, local copies, waits for them, and re-layouts, on_device(): jnp.einsum('tkd,khd->tkh', gradient_fragments, masked, preferred_element_...  13.5 us
    dot_general x1, matrix products, on_device(): jnp.einsum('tkd,khd->tkh', gradient_fragments, masked, preferred_element_...  12.9 us
    ppermute x4, waiting for transfers between devices, register_record(): lax.ppermute(raw_out, axis_name, list(map(lambda j: (j, (j + 1) % piece_o...  12.7 us
    all_gather x1, waiting for transfers between devices, on_device(): lax.all_gather(weight_slots, 'dp', axis=1, tiled=True)[0]  12.6 us
    ppermute x3, starting transfers between devices, register_record(): lax.ppermute(low, axis_name, list(map(lambda j: (j, (j - 1) % piece_out),...  11.4 us
    dot_general x1, matrix products, on_device(): jnp.einsum('tkh,tkd->khd', act_pieces, gradient_fragments, preferred_elem...  11.1 us
    gather x1, local copies, waits for them, and re-layouts, on_device(): act_pieces = act_blocks[:, row_ids, :]  10.5 us
  transfers between devices with their start and end apart: 9, of which 5 were waited for; matrix products, arithmetic and copies ran while one was open for 9% of the time, Pallas kernels for 0%

profile of v1, /device:TPU:0, one launch (start us, length us, event | category | flops | bytes accessed | tf_op | source)
XLA Modules:
  0.0 226.7 jit_solution(3703165426229686573)
XLA Ops:
  9.0 3.0 %collective-permute-start = (bf16[128,768]{0,1:T(8,128)(2,1)S(1)}, bf16[128,768]{0,1:T(8,128)(2,1)}, u32[]{:S(2)}, u32[]{:S(2)}) collective-permute-start(bf16[128,768]{0,1:T(8,128)(2,1)S(1)} %copy.20), channel_id=1, source_target_pairs={{0,1},{1,2},{2,3},{3,4},{4,5},{5,6},{6,7},{7,0},{8,9},{9,10},{10,1... | collective-permute-start | bytes 589832 | tf_op jit(solution)/shard_map/ppermute | solution.py:22
  12.1 3.1 %collective-permute-start.1 = (bf16[128,768]{0,1:T(8,128)(2,1)S(1)}, bf16[128,768]{0,1:T(8,128)(2,1)S(1)}, u32[]{:S(2)}, u32[]{:S(2)}) collective-permute-start(bf16[128,768]{0,1:T(8,128)(2,1)S(1)} %copy.20), channel_id=1, source_target_pairs={{0,7},{1,0},{2,1},{3,2},{4,3},{5,4},{6,5},{7,6},{8,15},{9,8},{10,9... | collective-permute-start | bytes 589832 | tf_op jit(solution)/shard_map/ppermute | solution.py:27
  20.0 5.1 %all-reduce.3 = (s32[292]{0:T(512)S(1)}, s32[4]{0:T(128)S(1)}, s32[292]{0:T(512)S(1)}) all-reduce(s32[292]{0:T(512)S(1)} %bitcast_dynamic-update-slice_fusion, s32[4]{0:T(128)S(1)} %bitcast_dynamic-update-slice_fusion.1, s32[292]{0:T(512)S(1)} %bitcast_dynamic-update-slice_fusion.2), channel_id=1, replica_groups=mesh['dp'=4,'pipe'=8] {'dp'}, use_global_device_ids=true, to_apply=%add.2 | all-reduce | flops 588 | bytes 4704
  25.2 1.6 copy.25
  27.2 4.7 %collective-permute-start.3 = (bf16[128,768]{0,1:T(8,128)(2,1)S(1)}, bf16[128,768]{0,1:T(8,128)(2,1)S(1)}, u32[]{:S(2)}, u32[]{:S(2)}) collective-permute-start(bf16[128,768]{0,1:T(8,128)(2,1)S(1)} %collective-permute-done.1), channel_id=1, source_target_pairs={{0,7},{1,0},{2,1},{3,2},{4,3},{5,4},{6,5},{7,6},{8,15},{9,8},{10,9... | collective-permute-start | bytes 589832 | tf_op jit(solution)/shard_map/ppermute | solution.py:27
  32.9 3.3 %collective-permute-done.2 = bf16[128,768]{0,1:T(8,128)(2,1)S(1)} collective-permute-done((bf16[128,768]{0,1:T(8,128)(2,1)}, bf16[128,768]{0,1:T(8,128)(2,1)S(1)}, u32[]{:S(2)}, u32[]{:S(2)}) %collective-permute-start.2) | collective-permute-done | bytes 196640 | tf_op jit(solution)/shard_map/ppermute | solution.py:22
  36.2 1.7 collective-permute-start.4
  37.9 3.6 %collective-permute-start.5 = (bf16[128,768]{0,1:T(8,128)(2,1)S(1)}, bf16[128,768]{0,1:T(8,128)(2,1)S(1)}, u32[]{:S(2)}, u32[]{:S(2)}) collective-permute-start(bf16[128,768]{0,1:T(8,128)(2,1)S(1)} %collective-permute-done.3), channel_id=1, source_target_pairs={{0,7},{1,0},{2,1},{3,2},{4,3},{5,4},{6,5},{7,6},{8,15},{9,8},{10,9... | collective-permute-start | bytes 589832 | tf_op jit(solution)/shard_map/ppermute | solution.py:27
  41.5 3.6 %collective-permute-done.4 = bf16[128,768]{0,1:T(8,128)(2,1)S(1)} collective-permute-done((bf16[128,768]{0,1:T(8,128)(2,1)S(1)}, bf16[128,768]{0,1:T(8,128)(2,1)S(1)}, u32[]{:S(2)}, u32[]{:S(2)}) %collective-permute-start.4) | collective-permute-done | bytes 196640 | tf_op jit(solution)/shard_map/ppermute | solution.py:22
  45.1 2.5 %collective-permute-start.6 = (bf16[128,768]{0,1:T(8,128)(2,1)S(1)}, bf16[128,768]{0,1:T(8,128)(2,1)S(1)}, u32[]{:S(2)}, u32[]{:S(2)}) collective-permute-start(bf16[128,768]{0,1:T(8,128)(2,1)S(1)} %collective-permute-done.4), channel_id=1, source_target_pairs={{0,1},{1,2},{2,3},{3,4},{4,5},{5,6},{6,7},{7,0},{8,9},{9,10},{10,1... | collective-permute-start | bytes 589832 | tf_op jit(solution)/shard_map/ppermute | solution.py:22
  47.7 5.8 %collective-permute-done.6 = bf16[128,768]{0,1:T(8,128)(2,1)S(1)} collective-permute-done((bf16[128,768]{0,1:T(8,128)(2,1)S(1)}, bf16[128,768]{0,1:T(8,128)(2,1)S(1)}, u32[]{:S(2)}, u32[]{:S(2)}) %collective-permute-start.6) | collective-permute-done | bytes 196640 | tf_op jit(solution)/shard_map/ppermute | solution.py:22
  54.4 10.5 %gather_fusion = bf16[292,128,128]{2,1,0:T(8,128)(2,1)} fusion(bf16[128,48,128]{2,0,1:T(8,128)(2,1)S(1)} %copy.23, s32[1024]{0:T(1024)S(1)} %pad_clamp_fusion.1), kind=kCustom, calls=%fused_computation | custom fusion | bytes 19137680 | tf_op jit(solution)/shard_map/gather | solution.py:60
  64.9 12.6 %all-gather.2.cloned.1.call-done = bf16[1,292,128,128]{3,2,0,1:T(8,128)(2,1)} async-done(((bf16[1,73,128,128]{3,2,0,1:T(8,128)(2,1)}), bf16[1,292,128,128]{3,2,0,1:T(8,128)(2,1)}) %all-gather.2.cloned.1.call-update) | async-done | bytes 9568272 | tf_op jit(solution)/shard_map/all_gather | solution.py:62
  77.4 12.9 %fusion.5 = bf16[128,292,128]{0,2,1:T(8,128)(2,1)} fusion(bf16[292,128,128]{2,1,0:T(8,128)(2,1)} %gather_fusion, bf16[1,292,128,128]{3,2,0,1:T(8,128)(2,1)} %all-gather.2.cloned.1.call-done, bf16[292]{0:T(512)(128)(2,1)S(1)} %convert_element_type.27), kind=kOutput, calls=%fused_computation.9 | convolution fusion | flops 1229520896 | bytes 28705352 | tf_op jit(solution)/shard_map/tkd,khd->tkh/dot_general | solution.py:65
  90.3 13.5 %copy.24 = bf16[128,292,128]{2,1,0:T(8,128)(2,1)} copy(bf16[128,292,128]{0,2,1:T(8,128)(2,1)} %fusion.5) | data formatting | bytes 19136512 | tf_op jit(solution)/shard_map/tkd,khd->tkh/transpose | solution.py:65
  103.9 7.4 %convolution_bitcast_fusion = f32[128,48,128]{2,1,0:T(8,128)} fusion(bf16[128,292,128]{2,1,0:T(8,128)(2,1)} %copy.24, s32[292]{0:T(512)S(1)} %copy-done.3), kind=kOutput, calls=%fused_computation.25 | convolution fusion | flops 459290304 | bytes 12715152 | tf_op jit(solution)/shard_map/tkh,kr->trh/dot_general | solution.py:69
  111.3 2.4 %copy.31 = f32[128,48,128]{0,2,1:T(8,128)S(1)} copy(f32[128,48,128]{2,1,0:T(8,128)} %convolution_bitcast_fusion) | data formatting | bytes 6291456 | tf_op jit(solution)/shard_map/reshape | solution.py:85
  113.7 3.9 %fusion.21 = (bf16[128,6144]{0,1:T(8,128)(2,1)}, bf16[128,6144]{0,1:T(8,128)(2,1)}) fusion(bf16[128,6144]{0,1:T(8,128)(2,1)} %copy.25, f32[128,48,128]{0,2,1:T(8,128)S(1)} %copy.31), kind=kLoop, calls=%fused_computation.24 | loop fusion | flops 10223616 | bytes 7864320 | tf_op jit(solution)/shard_map/convert_element_type | solution.py:48
  117.7 1.9 copy.27
  119.6 10.5 %gather_fusion.1 = bf16[292,128,128]{2,1,0:T(8,128)(2,1)} fusion(bf16[128,48,128]{2,0,1:T(8,128)(2,1)S(1)} %copy.27, s32[1024]{0:T(1024)S(1)} %pad_clamp_fusion), kind=kCustom, calls=%fused_computation.1 | custom fusion | bytes 19137680 | tf_op jit(solution)/shard_map/gather | solution.py:73
  130.0 11.1 %multiply_convert_fusion = bf16[292,128,128]{2,1,0:T(8,128)(2,1)} fusion(f32[292]{0:T(512)S(1)} %get-tuple-element.9, bf16[292,128,128]{2,1,0:T(8,128)(2,1)} %gather_fusion, bf16[292,128,128]{2,1,0:T(8,128)(2,1)} %gather_fusion.1), kind=kOutput, calls=%fused_computation.2 | convolution fusion | flops 1234305024 | bytes 28705936 | tf_op jit(solution)/shard_map/tkh,tkd->khd/dot_general | solution.py:75
  141.1 1.4 copy-done
  142.5 1.6 copy.29
  144.1 75.8 %reduce-scatter.2.cloned.1.call-done = bf16[73,128,128]{2,1,0:T(8,128)(2,1)} async-done(((bf16[292,128,128]{2,1,0:T(8,128)(2,1)}), bf16[73,128,128]{2,1,0:T(8,128)(2,1)}) %reduce-scatter.2.cloned.1.call-update) | async-done | bytes 2392080 | tf_op jit(solution)/shard_map/reduce_scatter | solution.py:78
  (42 shorter events, 7.9 us)
Async XLA Ops:
  7.2 18.0 %copy-start.1 = (bf16[128,6144]{1,0:T(8,128)(2,1)S(1)}, bf16[128,6144]{1,0:T(8,128)(2,1)}, u32[]{:S(2)}) copy-start(bf16[128,6144]{1,0:T(8,128)(2,1)} %param.6) | copy-start | bytes 4718596
  7.2 70.3 %all-gather.2.cloned.1.call-start = ((), (), s32[]{:S(2)}) async-start(), calls=%async_computation.1 | async-start | bytes 11960320 | tf_op jit(solution)/shard_map/all_gather | solution.py:62
  7.9 212.0 %reduce-scatter.2.cloned.1.call-start = ((), (), s32[]{:S(2)}) async-start(), calls=%async_computation.2 | async-start | bytes 11960320 | tf_op jit(solution)/shard_map/reduce_scatter | solution.py:78
  9.0 18.1 %collective-permute-start = (bf16[128,768]{0,1:T(8,128)(2,1)S(1)}, bf16[128,768]{0,1:T(8,128)(2,1)}, u32[]{:S(2)}, u32[]{:S(2)}) collective-permute-start(bf16[128,768]{0,1:T(8,128)(2,1)S(1)} %copy.20), channel_id=1, source_target_pairs={{0,1},{1,2},{2,3},{3,4},{4,5},{5,6},{6,7},{7,0},{8,9},{9,10},{10,1... | collective-permute-start | bytes 589832 | tf_op jit(solution)/shard_map/ppermute | solution.py:22
  12.1 15.1 %collective-permute-start.1 = (bf16[128,768]{0,1:T(8,128)(2,1)S(1)}, bf16[128,768]{0,1:T(8,128)(2,1)S(1)}, u32[]{:S(2)}, u32[]{:S(2)}) collective-permute-start(bf16[128,768]{0,1:T(8,128)(2,1)S(1)} %copy.20), channel_id=1, source_target_pairs={{0,7},{1,0},{2,1},{3,2},{4,3},{5,4},{6,5},{7,6},{8,15},{9,8},{10,9... | collective-permute-start | bytes 589832 | tf_op jit(solution)/shard_map/ppermute | solution.py:27
  25.0 1.8 copy-start.2
  27.1 9.0 %collective-permute-start.2 = (bf16[128,768]{0,1:T(8,128)(2,1)}, bf16[128,768]{0,1:T(8,128)(2,1)S(1)}, u32[]{:S(2)}, u32[]{:S(2)}) collective-permute-start(bf16[128,768]{0,1:T(8,128)(2,1)} %collective-permute-done), channel_id=1, source_target_pairs={{0,1},{1,2},{2,3},{3,4},{4,5},{5,6},{6,7},{7,0},{8,9},{9,10},{10,1... | collective-permute-start | bytes 589832 | tf_op jit(solution)/shard_map/ppermute | solution.py:22
  27.2 10.7 %collective-permute-start.3 = (bf16[128,768]{0,1:T(8,128)(2,1)S(1)}, bf16[128,768]{0,1:T(8,128)(2,1)S(1)}, u32[]{:S(2)}, u32[]{:S(2)}) collective-permute-start(bf16[128,768]{0,1:T(8,128)(2,1)S(1)} %collective-permute-done.1), channel_id=1, source_target_pairs={{0,7},{1,0},{2,1},{3,2},{4,3},{5,4},{6,5},{7,6},{8,15},{9,8},{10,9... | collective-permute-start | bytes 589832 | tf_op jit(solution)/shard_map/ppermute | solution.py:27
  36.2 8.9 %collective-permute-start.4 = (bf16[128,768]{0,1:T(8,128)(2,1)S(1)}, bf16[128,768]{0,1:T(8,128)(2,1)S(1)}, u32[]{:S(2)}, u32[]{:S(2)}) collective-permute-start(bf16[128,768]{0,1:T(8,128)(2,1)S(1)} %collective-permute-done.2), channel_id=1, source_target_pairs={{0,1},{1,2},{2,3},{3,4},{4,5},{5,6},{6,7},{7,0},{8,9},{9,10},{10,1... | collective-permute-start | bytes 589832 | tf_op jit(solution)/shard_map/ppermute | solution.py:22
  37.9 9.8 %collective-permute-start.5 = (bf16[128,768]{0,1:T(8,128)(2,1)S(1)}, bf16[128,768]{0,1:T(8,128)(2,1)S(1)}, u32[]{:S(2)}, u32[]{:S(2)}) collective-permute-start(bf16[128,768]{0,1:T(8,128)(2,1)S(1)} %collective-permute-done.3), channel_id=1, source_target_pairs={{0,7},{1,0},{2,1},{3,2},{4,3},{5,4},{6,5},{7,6},{8,15},{9,8},{10,9... | collective-permute-start | bytes 589832 | tf_op jit(solution)/shard_map/ppermute | solution.py:27
  45.1 8.4 %collective-permute-start.6 = (bf16[128,768]{0,1:T(8,128)(2,1)S(1)}, bf16[128,768]{0,1:T(8,128)(2,1)S(1)}, u32[]{:S(2)}, u32[]{:S(2)}) collective-permute-start(bf16[128,768]{0,1:T(8,128)(2,1)S(1)} %collective-permute-done.4), channel_id=1, source_target_pairs={{0,1},{1,2},{2,3},{3,4},{4,5},{5,6},{6,7},{7,0},{8,9},{9,10},{10,1... | collective-permute-start | bytes 589832 | tf_op jit(solution)/shard_map/ppermute | solution.py:22
  90.3 13.5 %copy-start.3 = (s32[292]{0:T(512)S(1)}, s32[292]{0:T(512)}, u32[]{:S(2)}) copy-start(s32[292]{0:T(512)} %copy-done.2) | copy-start | bytes 3508
  141.1 1.4 copy-start
Sparse Core Ops, SparseCore 0:
  9.5 67.8 all-gather.1
  141.3 78.5 reduce-scatter.1
